TPU v7x, 32 devices: a whole 2x2x4 slice. The times are simulated.
32 devices in a mesh: group: 2 (over x), seq: 16 (over z, y, core).
Axes of the slice: x: 2, y: 2, z: 4, core: 2. Of those that a mesh axis runs over, the one named last changes fastest.
Arguments:
- tokens: bfloat16 [16384, 2048], P(('group', 'seq')), parts along dimension 0, may hold values from -6 to 6
- w_qkv: bfloat16 [2048, 3072], P('seq'), may hold values from -0.125 to 0.125
- w_out: bfloat16 [1024, 2048], P('seq'), may hold values from -0.1875 to 0.1875
- level_weight: float32 [14, 4, 16384], P(None, None, ('group', 'seq')), parts along dimension 2, may hold values from 0.1 to 1
Outputs:
- mixed: bfloat16 [16384, 2048], P(('group', 'seq')), parts along dimension 0
There are 2 independent parts, one for each index of `group`. A program takes and returns all parts, laid end to end along the dimension named above; an argument that names none is the same for every part. Nothing has to cross between parts.
All inputs are finite; a program needn't handle non-finite values.
Results may differ from a plain program's by a relative error of at most 0.0085.
Values may be sent and summed in bfloat16 or wider, within the bound.
A program may use at most 128 MiB of HBM per device.

v0:
```python
import math

import jax
import jax.numpy as jnp
from jax import lax
from jax.sharding import PartitionSpec as P

HEADS = 4
HEAD = 256
SPAN = 256
CBITS = 8


def partner_2(value, axis, bit):
    mask = 2**bit
    pairs = [(source, source ^ mask) for source in range(lax.axis_size(axis))]
    return lax.ppermute(value, axis, pairs)


def bit_length_of(values):
    result = jnp.zeros(values.shape, jnp.int32)
    for bit_pos in range(24):
        result = result + (values >= 1 << bit_pos).astype(jnp.int32)
    return result


def intra_table(span, cbits, head):
    position = jnp.arange(span, dtype=jnp.int32)
    pair_level = bit_length_of(position[:, None] ^ position[None, :])
    causal = position[:, None] >= position[None, :]
    levels_all = jnp.arange(cbits + 1, dtype=jnp.int32)
    gains = jnp.asarray(
        [1.0 / math.sqrt(head * max(1, 2 ** (level_no - 1))) for level_no in range(cbits + 1)],
        jnp.float32,
    )
    onehot = ((pair_level[None] == levels_all[:, None, None]) & causal[None]).astype(jnp.float32)
    return onehot * gains[:, None, None]


def split_read(form, query_half, state):
    upper_part = state.astype(jnp.bfloat16)
    lower_part = (state - upper_part.astype(jnp.float32)).astype(jnp.bfloat16)
    first = jnp.einsum(form, query_half, upper_part, preferred_element_type=jnp.float32)
    second = jnp.einsum(form, query_half, lower_part, preferred_element_type=jnp.float32)
    return first + second


def on_device(tokens, w_qkv, w_out, level_weight):
    highest = lax.Precision.HIGHEST
    head_cols = HEADS * HEAD
    tok_rows = tokens.shape[0]
    count = tok_rows // SPAN
    columns = tokens
    qkv = jnp.dot(
        columns,
        lax.all_gather(w_qkv, "seq", axis=0, tiled=True),
        preferred_element_type=jnp.float32,
    ).astype(jnp.bfloat16)
    queries = qkv[:, :head_cols].reshape(count, SPAN, HEADS, HEAD)
    key_rows = qkv[:, head_cols : 2 * head_cols].reshape(count, SPAN, HEADS, HEAD)
    value_rows = qkv[:, 2 * head_cols :].reshape(count, SPAN, HEADS, HEAD)
    weights = level_weight.reshape(level_weight.shape[0], HEADS, count, SPAN)
    table = intra_table(SPAN, CBITS, HEAD)
    mixing = jnp.einsum("lij,lhci->chij", table, weights[: CBITS + 1], precision=highest)
    scores = jnp.einsum("cihe,cjhe->chij", queries, key_rows, preferred_element_type=jnp.float32)
    probs = (scores * mixing).astype(jnp.bfloat16)
    intra = jnp.einsum("chij,cjhe->cihe", probs, value_rows, preferred_element_type=jnp.float32)
    states = jnp.einsum("cjhe,cjhf->chef", key_rows, value_rows, preferred_element_type=jnp.float32)
    inter = jnp.zeros((count, SPAN, HEADS, HEAD), jnp.float32)
    local_bits = count.bit_length() - 1
    level_no = 1
    half_size = 2 ** (level_no - 1)
    blocks = count // (2 * half_size)
    left = states.reshape(blocks, 2, half_size, HEADS, HEAD, HEAD)[:, 0].sum(axis=1)
    right_q = queries.reshape(blocks, 2, half_size, SPAN, HEADS, HEAD)[:, 1]
    read = split_read("bmihe,bhef->bmihf", right_q, left)
    scale = weights[CBITS + level_no].reshape(HEADS, blocks, 2, half_size, SPAN)[:, :, 1]
    scale = jnp.transpose(scale, (1, 2, 3, 0)) * (1.0 / math.sqrt(SPAN * half_size * HEAD))
    shaped = inter.reshape(blocks, 2, half_size, SPAN, HEADS, HEAD)
    inter = shaped.at[:, 1].add(read * scale[..., None]).reshape(count, SPAN, HEADS, HEAD)
    block_total = states.sum(axis=0)
    seq_bits = lax.axis_size("seq").bit_length() - 1
    device = lax.axis_index("seq")
    for bit_pos in range(seq_bits):
        upper = (device >> bit_pos & 1).astype(jnp.float32)
        partner = partner_2(block_total, "seq", bit_pos)
        level_no = local_bits + bit_pos + 1
        gain = 1.0 / math.sqrt(SPAN * 2 ** (level_no - 1) * HEAD)
        level_scale = jnp.transpose(weights[CBITS + level_no], (1, 2, 0)) * (upper * gain)
        single = split_read("cihe,hef->cihf", queries, partner)
        inter = inter + single * level_scale[..., None]
        if bit_pos + 1 < seq_bits:
            block_total = block_total + partner
    attended = (intra + inter).reshape(tok_rows, head_cols).astype(jnp.bfloat16)
    columns = attended
    mixed = jnp.dot(
        columns,
        lax.all_gather(w_out, "seq", axis=0, tiled=True),
        preferred_element_type=jnp.float32,
    )
    return mixed.astype(jnp.bfloat16)


def solution(mesh):
    return jax.shard_map(
        on_device,
        mesh=mesh,
        in_specs=(
            P(("group", "seq"), None),
            P("seq", None),
            P("seq", None),
            P(None, None, ("group", "seq")),
        ),
        out_specs=P(("group", "seq"), None),
        check_vma=False,
    )
```

profile of v0, /device:TPU:0, one launch (start us, length us, event | category | flops | bytes accessed | tf_op | source)
XLA Modules:
  0.0 262.6 jit_solution(4871203415658004380)
XLA Ops:
  6.5 0.0 copy-start
  6.5 0.0 all-gather.3.cloned.1.call-start
  6.5 0.7 all-gather.3.cloned.1.call-update
  7.3 0.0 all-gather.5.cloned.1.call-start
  7.3 0.7 all-gather.5.cloned.1.call-update
  8.0 104.8 %all-gather.3.cloned.1.call-done = bf16[2048,3072]{1,0:T(8,128)(2,1)} async-done(((bf16[128,3072]{1,0:T(8,128)(2,1)}), bf16[2048,3072]{1,0:T(8,128)(2,1)}) %all-gather.3.cloned.1.call-update) | async-done | bytes 12582928 | tf_op jit(solution)/shard_map/all_gather | solution.py:56
  112.8 0.0 copy-done
  112.8 9.6 %convolution_convert_fusion = bf16[512,3072]{1,0:T(8,128)(2,1)S(1)} fusion(bf16[512,2048]{1,0:T(8,128)(2,1)S(1)} %copy-done, bf16[2048,3072]{1,0:T(8,128)(2,1)} %all-gather.3.cloned.1.call-done), kind=kOutput, calls=%fused_computation | convolution fusion | flops 6444023808 | bytes 17825792 | tf_op jit(solution)/shard_map/dot_general | solution.py:54
  122.4 1.3 fusion.89
  123.7 0.8 reshape.219
  124.5 0.7 copy.99
  125.2 0.8 reshape.217
  126.0 1.8 fusion.90
  127.8 1.4 copy.101
  129.2 0.3 collective-permute-start
  129.5 0.8 convert_add_fusion
  130.3 0.0 copy-done.9
  130.3 0.0 copy-start.10
  130.3 1.8 collective-permute-done
  132.1 2.8 %add.256 = f32[4,256,256]{1,2,0:T(8,128)} add(f32[4,256,256]{1,2,0:T(8,128)} %copy.101, f32[4,256,256]{1,2,0:T(8,128)S(1)} %collective-permute-done) | non-fusion elementwise | flops 262144 | bytes 3145728 | tf_op jit(solution)/shard_map/add | solution.py:93
  134.9 0.6 collective-permute-start.1
  135.5 0.0 slice-done
  135.5 0.1 slice.83
  135.6 1.3 copy.96
  136.9 0.0 copy-done.2
  136.9 0.0 copy-done.10
  136.9 8.4 %fusion = f32[256,256,4,2]{1,2,3,0:T(4,128)} fusion(f32[9,4,2,256]{0,1,2,3:T(4,128)} %copy.96, f32[9]{0:T(128)S(1)} %copy-done.10, s32[256,256]{1,0:T(8,128)} %convert_add_fusion, pred[256,256]{1,0:T(8,128)(4,1)S(1)} %iota_compare_fusion.1), kind=kOutput, calls=%fused_computation.1 | convolution fusion | flops 58392576 | bytes 2498596 | tf_op jit(solution)/shard_map/lij,lhci->chij/dot_general | solution.py:64
  145.3 1.9 reshape.218
  147.2 2.6 %reshape_reshape.3 = bf16[1,2,1,256,4,256]{5,4,3,1,2,0:T(4,128)(2,1)} reshape(bf16[512,1024]{1,0:T(8,128)(2,1)} %get-tuple-element.17) | data formatting | bytes 2097152 | tf_op jit(solution)/shard_map/reshape;reshape | solution.py:75
  149.8 1.2 slice.96
  151.0 0.0 copy-start.6
  151.0 0.8 copy-done.6
  151.9 2.5 fusion.42
  154.4 4.2 %fusion.15 = f32[2,4,256,256]{3,2,1,0:T(8,128)} fusion(f32[256,256,4,2]{1,2,3,0:T(4,128)} %fusion, bf16[2,256,4,256]{1,3,2,0:T(8,128)(2,1)S(1)} %copy.99, bf16[2,256,4,256]{3,2,1,0:T(4,128)(2,1)S(1)} %reshape.217, bf16[2,256,4,256]{3,2,1,0:T(4,128)(2,1)S(1)} %reshape.218), kind=kOutput, calls=%fused_computation.22 | convolution fusion | flops 537919488 | bytes 7340032 | tf_op jit(solution)/shard_map/chij,cjhe->cihe/dot_general | solution.py:67
  158.6 13.2 %collective-permute-done.1 = f32[4,256,256]{1,2,0:T(8,128)} collective-permute-done((f32[4,256,256]{1,2,0:T(8,128)}, f32[4,256,256]{1,2,0:T(8,128)}, u32[]{:S(2)}, u32[]{:S(2)}) %collective-permute-start.1) | collective-permute-done | bytes 1048608 | tf_op jit(solution)/shard_map/ppermute | solution.py:17
  171.8 1.7 add.260
  173.5 0.5 collective-permute-start.2
  174.0 0.0 copy-done.3
  174.0 0.5 fusion.25
  174.4 0.0 copy-start.5
  174.4 0.0 copy-start.7
  174.5 0.0 copy-start.8
  174.5 0.5 bitcast_multiply_fusion.3
  175.0 1.1 copy-done.5
  176.0 0.1 copy-done.7
  176.1 0.3 copy-done.8
  176.4 0.5 fusion.19
  177.0 21.0 %collective-permute-done.2 = f32[4,256,256]{1,2,0:T(8,128)S(1)} collective-permute-done((f32[4,256,256]{1,2,0:T(8,128)S(1)}, f32[4,256,256]{1,2,0:T(8,128)S(1)}, u32[]{:S(2)}, u32[]{:S(2)}) %collective-permute-start.2) | collective-permute-done | bytes 1048608 | tf_op jit(solution)/shard_map/ppermute | solution.py:17
  198.0 0.1 add.264
  198.2 1.5 collective-permute-start.3
  199.7 1.7 fusion.39
  201.4 2.1 fusion.28
  203.5 0.5 fusion.37
  203.9 0.5 fusion.31
  204.4 0.0 copy-start.4
  204.4 40.6 %collective-permute-done.3 = f32[4,256,256]{1,2,0:T(8,128)S(1)} collective-permute-done((f32[4,256,256]{1,2,0:T(8,128)S(1)}, f32[4,256,256]{1,2,0:T(8,128)S(1)}, u32[]{:S(2)}, u32[]{:S(2)}) %collective-permute-start.3) | collective-permute-done | bytes 1048608 | tf_op jit(solution)/shard_map/ppermute | solution.py:17
  245.1 0.5 fusion.34
  245.6 0.0 copy-done.4
  245.6 2.3 fusion.7
  247.8 1.7 copy.127
  249.5 0.2 copy.156
  249.7 0.0 all-gather.5.cloned.1.call-done
  249.8 0.0 copy-start.1
  249.8 6.0 %convolution_convert_fusion.1 = bf16[512,2048]{1,0:T(8,128)(2,1)} fusion(bf16[512,1024]{1,0:T(8,128)(2,1)S(1)} %bitcast.123, bf16[1024,2048]{1,0:T(8,128)(2,1)} %all-gather.5.cloned.1.call-done), kind=kOutput, calls=%fused_computation.6 | convolution fusion | flops 2148532224 | bytes 7340032 | tf_op jit(solution)/shard_map/dot_general | solution.py:96
  (8 shorter events, 0.0 us)
Async XLA Ops:
  6.5 106.3 %copy-start = (bf16[512,2048]{1,0:T(8,128)(2,1)S(1)}, bf16[512,2048]{1,0:T(8,128)(2,1)}, u32[]{:S(2)}) copy-start(bf16[512,2048]{1,0:T(8,128)(2,1)} %param.7) | copy-start | bytes 6291460
  6.5 106.3 %all-gather.3.cloned.1.call-start = ((), (), s32[]{:S(2)}) async-start(), calls=%async_computation | async-start | bytes 13369344 | tf_op jit(solution)/shard_map/all_gather | solution.py:56
  7.3 242.5 %all-gather.5.cloned.1.call-start = ((), (), s32[]{:S(2)}) async-start(), calls=%async_computation.1 | async-start | bytes 4456448 | tf_op jit(solution)/shard_map/all_gather | solution.py:98
  127.8 2.5 copy-start.9
  129.2 6.3 %slice-start = ((f32[14,4,512]{2,1,0:T(4,128)}), f32[9,4,512]{2,1,0:T(4,128)S(1)}, s32[]{:S(2)}) async-start(f32[14,4,512]{2,1,0:T(4,128)} %param.10), calls=%async_computation.2 | async-start | bytes 147456 | tf_op jit(solution)/shard_map/slice | solution.py:64
  129.2 2.9 %collective-permute-start = (f32[4,256,256]{1,2,0:T(8,128)}, f32[4,256,256]{1,2,0:T(8,128)S(1)}, u32[]{:S(2)}, u32[]{:S(2)}) collective-permute-start(f32[4,256,256]{1,2,0:T(8,128)} %copy.101), channel_id=1, source_target_pairs={{0,1},{1,0},{2,3},{3,2},{4,5},{5,4},{6,7},{7,6},{8,9},{9,8},{10,11... | collective-permute-start | bytes 3145736 | tf_op jit(solution)/shard_map/ppermute | solution.py:17
  130.3 6.6 %copy-start.10 = (f32[9]{0:T(128)S(1)}, f32[9]{0:T(128)}, u32[]{:S(2)}) copy-start(f32[9]{0:T(128)} %constant.101.clone) | copy-start | bytes 112
  132.1 4.8 %copy-start.2 = (f32[4,256,256]{1,2,0:T(8,128)}, f32[4,256,256]{1,2,0:T(8,128)S(1)}, u32[]{:S(2)}) copy-start(f32[4,256,256]{1,2,0:T(8,128)S(1)} %collective-permute-done) | copy-start | bytes 3145732
  134.9 36.9 %collective-permute-start.1 = (f32[4,256,256]{1,2,0:T(8,128)}, f32[4,256,256]{1,2,0:T(8,128)}, u32[]{:S(2)}, u32[]{:S(2)}) collective-permute-start(f32[4,256,256]{1,2,0:T(8,128)} %add.256), channel_id=1, source_target_pairs={{0,2},{1,3},{2,0},{3,1},{4,6},{5,7},{6,4},{7,5},{8,10},{9,11},{10,... | collective-permute-start | bytes 3145736 | tf_op jit(solution)/shard_map/ppermute | solution.py:17
  151.0 0.9 copy-start.6
  158.6 15.3 %copy-start.3 = (f32[4,256,256]{1,2,0:T(8,128)S(1)}, f32[4,256,256]{1,2,0:T(8,128)}, u32[]{:S(2)}) copy-start(f32[4,256,256]{1,2,0:T(8,128)} %copy-done.2) | copy-start | bytes 3145732
  173.5 24.6 %collective-permute-start.2 = (f32[4,256,256]{1,2,0:T(8,128)S(1)}, f32[4,256,256]{1,2,0:T(8,128)S(1)}, u32[]{:S(2)}, u32[]{:S(2)}) collective-permute-start(f32[4,256,256]{1,2,0:T(8,128)S(1)} %add.260), channel_id=1, source_target_pairs={{0,4},{1,5},{2,6},{3,7},{4,0},{5,1},{6,2},{7,3},{8,12},{9,13},{10,... | collective-permute-start | bytes 3145736 | tf_op jit(solution)/shard_map/ppermute | solution.py:17
  174.4 1.6 copy-start.5
  174.4 1.7 copy-start.7
  174.5 2.0 copy-start.8
  198.2 46.9 %collective-permute-start.3 = (f32[4,256,256]{1,2,0:T(8,128)S(1)}, f32[4,256,256]{1,2,0:T(8,128)S(1)}, u32[]{:S(2)}, u32[]{:S(2)}) collective-permute-start(f32[4,256,256]{1,2,0:T(8,128)S(1)} %add.264), channel_id=1, source_target_pairs={{0,8},{1,9},{2,10},{3,11},{4,12},{5,13},{6,14},{7,15},{8,0},{9,1},... | collective-permute-start | bytes 3145736 | tf_op jit(solution)/shard_map/ppermute | solution.py:17
  204.4 41.1 %copy-start.4 = (f32[2,4,256,256]{3,2,1,0:T(8,128)S(1)}, f32[2,4,256,256]{3,2,1,0:T(8,128)}, u32[]{:S(2)}) copy-start(f32[2,4,256,256]{3,2,1,0:T(8,128)} %fusion.15) | copy-start | bytes 6291460
  249.8 6.0 %copy-start.1 = (bf16[512,2048]{1,0:T(8,128)(2,1)S(1)}, bf16[512,2048]{1,0:T(8,128)(2,1)}, u32[]{:S(2)}) copy-start(bf16[512,2048]{1,0:T(8,128)(2,1)} %param.7) | copy-start | bytes 6291460
Sparse Core Ops, SparseCore 0:
  9.6 103.1 all-gather.2
  115.0 60.1 all-gather.4
where the time goes:
time: 263 us
  waiting for transfers between devices  183 us (70%)
  matrix products  41.5 us (16%)
  local copies, waits for them, and re-layouts  16.3 us (6%)
  between operations  13.6 us (5%)
  other arithmetic  5.45 us (2%)
  starting transfers between devices  2.87 us (1%)
    all_gather x1, waiting for transfers between devices, on_device(): lax.all_gather(w_qkv, 'seq', axis=0, tiled=True)  105 us
    ppermute x4, waiting for transfers between devices, partner_2(): return lax.ppermute(value, axis, pairs)  76.6 us
    dot_general x1, matrix products, on_device(): jnp.dot(columns, lax.all_gather(w_qkv, 'seq', axis=0, tiled=True), prefer...  9.63 us
    dot_general x1, matrix products, on_device(): jnp.einsum('lij,lhci->chij', table, weights[:CBITS + 1], precision=highest)  8.37 us
    dot_general x5, matrix products, split_read(): jnp.einsum(form, query_half, upper_part, preferred_element_type=jnp.float32)  7.49 us
    dot_general x1, matrix products, on_device(): jnp.dot(columns, lax.all_gather(w_out, 'seq', axis=0, tiled=True), prefer...  5.99 us
  transfers between devices with their start and end apart: 6, of which 5 were waited for; matrix products, arithmetic and copies ran while one was open for 21% of the time, Pallas kernels for 0%

commit v1 on v0

--- a/solution.py
+++ b/solution.py
@@ -1,14 +1,238 @@
+import functools
 import math
 
 import jax
 import jax.numpy as jnp
 from jax import lax
+from jax.experimental import pallas as pl
+from jax.experimental.pallas import tpu as pltpu
 from jax.sharding import PartitionSpec as P
 
 HEADS = 4
 HEAD = 256
 SPAN = 256
 CBITS = 8
+MESH = pl.DeviceIdType.MESH
+
+
+class Place:
+    def __init__(self, groups, seqs):
+        self.seqs = seqs
+        self.chips = seqs // 2
+        self.has_x = groups % 2 == 0
+        self.g = lax.axis_index("group")
+        self.me = lax.axis_index("seq")
+        self.core = lax.rem(self.me, 2)
+        self.chip = self.me // 2
+        odd = lax.rem(self.chip, 2)
+        half = self.chip // 2
+        self.pos = half + odd * (self.chips - 1 - 2 * half)
+        self.par = lax.rem(self.g, 2)
+        self.mate = (self.g, self.me + 1 - 2 * self.core)
+        self.cross = (self.g + 1 - 2 * self.par, self.me)
+
+    def chip_at(self, offset):
+        pos = lax.rem(self.pos + offset + self.chips, self.chips)
+        late = pos // (self.chips // 2)
+        return 2 * pos + late * (2 * (self.chips - 1) + 1 - 4 * pos)
+
+    def ring(self, offset):
+        return (self.g, self.chip_at(offset) * 2 + self.core)
+
+    def greet(self, others):
+        barrier = pltpu.get_barrier_semaphore()
+        for other in others:
+            pl.semaphore_signal(barrier, inc=1, device_id=other, device_id_type=MESH)
+        pl.semaphore_wait(barrier, len(others))
+
+    def neighbours(self):
+        found = [self.ring(1), self.ring(-1), self.mate]
+        return found + [self.cross] if self.has_x else found
+
+
+def relay_columns(columns, has_x, share):
+    return (columns // share) // 128 * 128 if has_x else 0
+
+
+class Gather:
+    def __init__(self, place, buf, send_sem, recv_sem, share):
+        self.at = place
+        self.buf = buf
+        self.send_sem, self.recv_sem = send_sem, recv_sem
+        _, self.rows, self.columns = buf.shape
+        self.sub = 2 if self.rows % 32 == 0 else 1
+        self.part = self.rows // self.sub
+        self.rel = relay_columns(self.columns, place.has_x, share)
+        self.slots, self.sent = {}, []
+        keep = self.columns - self.rel
+        self.ring_cols = (place.par * self.rel, keep) if self.rel else (0, keep)
+        self.give_cols = (place.par * keep, self.rel)
+        self.take_cols = ((1 - place.par) * keep, self.rel)
+        self.last = place.chips // 2
+
+    def view(self, index, h, cols):
+        start, width = cols
+        if not isinstance(start, int):
+            start = pl.multiple_of(start, 128)
+        return self.buf.at[index, pl.ds(h * self.part, self.part), pl.ds(start, width)]
+
+    def copy(self, key, index, h, cols, device):
+        slot = self.slots.setdefault(key, len(self.slots))
+        ref = self.view(index, h, cols)
+        return pltpu.make_async_remote_copy(
+            src_ref=ref,
+            dst_ref=ref,
+            send_sem=self.send_sem.at[slot],
+            recv_sem=self.recv_sem.at[slot],
+            device_id=device,
+            device_id_type=MESH,
+        )
+
+    def send(self, *args):
+        one = self.copy(*args)
+        one.start()
+        self.sent.append(one)
+
+    def mine(self, offset):
+        return self.at.chip_at(offset) * 2 + self.at.core
+
+    def theirs(self, offset):
+        return self.at.chip_at(offset) * 2 + 1 - self.at.core
+
+    def pieces(self, step):
+        every = [(h, d) for h in range(self.sub) for d in (1, -1)]
+        if step < self.last:
+            return every
+        return [(0, 1), (1, -1)] if self.sub == 2 else [(0, 1)]
+
+    def begin(self):
+        for h, d in self.pieces(1):
+            self.send(("ring", 1, h, d), self.at.me, h, self.ring_cols, self.at.ring(d))
+        for h in range(self.sub):
+            self.send(("own", h), self.at.me, h, (0, self.columns), self.at.mate)
+
+    def own(self):
+        for h in range(self.sub):
+            self.copy(("own", h), self.theirs(0), h, (0, self.columns), self.at.mate).wait_recv()
+
+    def arrive(self, step):
+        for h, d in self.pieces(step):
+            index = self.mine(-d * step)
+            self.copy(("ring", step, h, d), index, h, self.ring_cols, self.at.ring(-d)).wait_recv()
+            if step < self.last and (h, d) in self.pieces(step + 1):
+                self.send(("ring", step + 1, h, d), index, h, self.ring_cols, self.at.ring(d))
+            if step < self.last and self.rel:
+                self.send(("cross", step, h, d), index, h, self.give_cols, self.at.cross)
+            self.send(("mate", step, h, d), index, h, self.ring_cols, self.at.mate)
+
+    def complete(self, step):
+        if self.rel:
+            for h, d in self.pieces(step):
+                index = self.mine(-d * step)
+                if step < self.last:
+                    self.copy(("cross", step, h, d), index, h, self.take_cols, self.at.cross).wait_recv()
+                    if step + 1 == self.last and (h, d) in self.pieces(step + 1):
+                        self.send(("end", h, d), index, h, self.take_cols, self.at.ring(d))
+                else:
+                    self.copy(("end", h, d), index, h, self.take_cols, self.at.ring(-d)).wait_recv()
+                self.send(("pass", step, h, d), index, h, self.take_cols, self.at.mate)
+        for h, d in self.pieces(step):
+            index = self.theirs(-d * step)
+            self.copy(("mate", step, h, d), index, h, self.ring_cols, self.at.mate).wait_recv()
+            if self.rel:
+                self.copy(("pass", step, h, d), index, h, self.take_cols, self.at.mate).wait_recv()
+        return (step, -step) if step < self.last else (step,)
+
+    def run(self, use):
+        self.own()
+        use(self.at.chip_at(0))
+        for step in range(1, self.last):
+            self.arrive(step)
+            if step > 1:
+                for offset in self.complete(step - 1):
+                    use(self.at.chip_at(offset))
+        for offset in self.complete(self.last - 1):
+            use(self.at.chip_at(offset))
+        self.arrive(self.last)
+        for offset in self.complete(self.last):
+            use(self.at.chip_at(offset))
+
+    def drain(self):
+        for one in self.sent:
+            one.wait_send()
+
+
+def slots_needed(seqs):
+    return 16 * seqs
+
+
+def project_kernel(groups, seqs, share, tokens_ref, w_ref, out_ref, buf, total, load_sem, send_sem, recv_sem):
+    place = Place(groups, seqs)
+    load = pltpu.make_async_copy(w_ref, buf.at[place.me], load_sem)
+    load.start()
+    place.greet(place.neighbours())
+    load.wait()
+    gather = Gather(place, buf, send_sem, recv_sem, share)
+    gather.begin()
+    rows, columns = w_ref.shape
+    tile = 512
+    aligned = (2 * rows) % 128 == 0
+    started = []
+
+    def use(chip):
+        if not aligned:
+            return
+        first = not started
+        started.append(1)
+        x = tokens_ref[:, pl.ds(pl.multiple_of(chip * (2 * rows), 128), 2 * rows)]
+
+        @pl.loop(0, columns // tile)
+        def _(t):
+            cols = pl.ds(pl.multiple_of(t * tile, tile), tile)
+            w = buf[pl.ds(chip * 2, 2), :, cols].reshape(2 * rows, tile)
+            y = jnp.dot(x, w, preferred_element_type=jnp.float32)
+            if first:
+                total[:, cols] = y
+            elif len(started) == place.chips:
+                out_ref[:, cols] = (total[:, cols] + y).astype(out_ref.dtype)
+            else:
+                total[:, cols] += y
+
+    gather.run(use)
+    if not aligned:
+
+        @pl.loop(0, columns // tile)
+        def _(t):
+            cols = pl.ds(pl.multiple_of(t * tile, tile), tile)
+            w = buf[:, :, cols].reshape(seqs * rows, tile)
+            y = jnp.dot(tokens_ref[...], w, preferred_element_type=jnp.float32)
+            out_ref[:, cols] = y.astype(out_ref.dtype)
+
+    gather.drain()
+
+
+def project(tokens, w, groups, seqs):
+    rows, columns = w.shape
+    count = tokens.shape[0]
+    return pl.pallas_call(
+        functools.partial(project_kernel, groups, seqs, 3),
+        out_shape=jax.ShapeDtypeStruct((count, columns), jnp.bfloat16),
+        in_specs=[
+            pl.BlockSpec(memory_space=pltpu.VMEM),
+            pl.BlockSpec(memory_space=pl.ANY),
+        ],
+        out_specs=pl.BlockSpec(memory_space=pltpu.VMEM),
+        scratch_shapes=[
+            pltpu.VMEM((seqs, rows, columns), jnp.bfloat16),
+            pltpu.VMEM((count, columns), jnp.float32),
+            pltpu.SemaphoreType.DMA,
+            pltpu.SemaphoreType.DMA((slots_needed(seqs),)),
+            pltpu.SemaphoreType.DMA((slots_needed(seqs),)),
+        ],
+        compiler_params=pltpu.CompilerParams(
+            collective_id=0, has_side_effects=True, vmem_limit_bytes=60 * 1024 * 1024
+        ),
+    )(tokens, w)
 
 
 def partner_2(value, axis, bit):
@@ -38,11 +262,7 @@
 
 
 def split_read(form, query_half, state):
-    upper_part = state.astype(jnp.bfloat16)
-    lower_part = (state - upper_part.astype(jnp.float32)).astype(jnp.bfloat16)
-    first = jnp.einsum(form, query_half, upper_part, preferred_element_type=jnp.float32)
-    second = jnp.einsum(form, query_half, lower_part, preferred_element_type=jnp.float32)
-    return first + second
+    return jnp.einsum(form, query_half, state.astype(jnp.bfloat16), preferred_element_type=jnp.float32)
 
 
 def on_device(tokens, w_qkv, w_out, level_weight):
@@ -50,12 +270,7 @@
     head_cols = HEADS * HEAD
     tok_rows = tokens.shape[0]
     count = tok_rows // SPAN
-    columns = tokens
-    qkv = jnp.dot(
-        columns,
-        lax.all_gather(w_qkv, "seq", axis=0, tiled=True),
-        preferred_element_type=jnp.float32,
-    ).astype(jnp.bfloat16)
+    qkv = project(tokens, w_qkv, lax.axis_size("group"), lax.axis_size("seq"))
     queries = qkv[:, :head_cols].reshape(count, SPAN, HEADS, HEAD)
     key_rows = qkv[:, head_cols : 2 * head_cols].reshape(count, SPAN, HEADS, HEAD)
     value_rows = qkv[:, 2 * head_cols :].reshape(count, SPAN, HEADS, HEAD)
@@ -83,7 +298,7 @@
     device = lax.axis_index("seq")
     for bit_pos in range(seq_bits):
         upper = (device >> bit_pos & 1).astype(jnp.float32)
-        partner = partner_2(block_total, "seq", bit_pos)
+        partner = partner_2(block_total.astype(jnp.bfloat16), "seq", bit_pos)
         level_no = local_bits + bit_pos + 1
         gain = 1.0 / math.sqrt(SPAN * 2 ** (level_no - 1) * HEAD)
         level_scale = jnp.transpose(weights[CBITS + level_no], (1, 2, 0)) * (upper * gain)

time: 263 us -> 192 us (0.73)
  waiting for transfers between devices: 183 us -> 40.8 us
  Pallas kernels: 0 us -> 86.2 us
  matrix products: 41.5 us -> 26.1 us
    all_gather x1 -> x0, waiting for transfers between devices: 105 us -> none  [on_device(): lax.all_gather(w_qkv, 'seq', axis=0, tiled=True)]
    pallas_call x0 -> x1, Pallas kernels: none -> 86.2 us  [project(): pl.pallas_call(functools.partial(project_kernel, groups, seqs, 3), out_sh...]
    ppermute x4, waiting for transfers between devices: 76.6 us -> 40.1 us  [partner_2(): return lax.ppermute(value, axis, pairs)]
    dot_general x11 -> x5, matrix products: 21.1 us -> 4.91 us  [split_read(): jnp.einsum(form, query_half, state.astype(jnp.bfloat16), preferred_elemen...]
    convert_element_type x0 -> x4, other arithmetic: none -> 5.67 us  [on_device(): partner = partner_2(block_total.astype(jnp.bfloat16), 'seq', bit_pos)]
    add x3 -> x0, other arithmetic: 4.61 us -> none  [on_device(): block_total = block_total + partner]
  transfers between devices with their start and end apart: 6 -> 5, of which waited for: 5 -> 3; matrix products, arithmetic and copies ran while one was open for 21% -> 21% of each run, Pallas kernels for 0% -> 45%
where the time goes in v1:
time: 192 us; the launch traced here: 191 us
  Pallas kernels  86.2 us (45%)
  waiting for transfers between devices  40.8 us (21%)
  matrix products  26.1 us (14%)
  local copies, waits for them, and re-layouts  14 us (7%)
  between operations  13.6 us (7%)
  other arithmetic  5.81 us (3%)
  starting transfers between devices  4.56 us (2%)
    pallas_call x1, Pallas kernels, project(): pl.pallas_call(functools.partial(project_kernel, groups, seqs, 3), out_sh...  86.2 us
    ppermute x4, waiting for transfers between devices, partner_2(): return lax.ppermute(value, axis, pairs)  40.1 us
    dot_general x1, matrix products, on_device(): jnp.einsum('lij,lhci->chij', table, weights[:CBITS + 1], precision=highest)  8.28 us
    dot_general x1, matrix products, on_device(): jnp.dot(columns, lax.all_gather(w_out, 'seq', axis=0, tiled=True), prefer...  5.85 us
    convert_element_type x4, other arithmetic, on_device(): partner = partner_2(block_total.astype(jnp.bfloat16), 'seq', bit_pos)  5.67 us
    dot_general x5, matrix products, split_read(): jnp.einsum(form, query_half, state.astype(jnp.bfloat16), preferred_elemen...  4.91 us
    dot_general x1, matrix products, on_device(): jnp.einsum('chij,cjhe->cihe', probs, value_rows, preferred_element_type=j...  4.56 us
    ppermute x4, starting transfers between devices, partner_2(): return lax.ppermute(value, axis, pairs)  4.56 us
  transfers between devices with their start and end apart: 5, of which 3 were waited for; matrix products, arithmetic and copies ran while one was open for 21% of the time, Pallas kernels for 45%

profile of v1, /device:TPU:0, one launch (start us, length us, event | category | flops | bytes accessed | tf_op | source)
XLA Modules:
  0.0 191.1 jit_solution(7106959665888077097)
XLA Ops:
  6.5 0.0 all-gather.2.cloned.1.call-start
  6.5 0.7 all-gather.2.cloned.1.call-update
  7.3 86.2 %shard_map.55 = bf16[512,3072]{1,0:T(8,128)(2,1)} custom-call(bf16[512,2048]{1,0:T(8,128)(2,1)} %tokens_ref.1, bf16[128,3072]{1,0:T(8,128)(2,1)} %w_ref.1), custom_call_target="tpu_custom_call" | custom-call | tf_op jit(solution)/shard_map/pallas_call | solution.py:217
  93.5 3.2 %fusion.62 = (bf16[512,1024]{1,0:T(8,128)(2,1)S(1)}, bf16[512,1024]{1,0:T(8,128)(2,1)S(1)}, bf16[512,1024]{1,0:T(8,128)(2,1)}) fusion(bf16[512,3072]{1,0:T(8,128)(2,1)} %shard_map.55), kind=kLoop, calls=%fused_computation.83 | loop fusion | bytes 6291456 | tf_op jit(solution)/shard_map/slice | solution.py:276
  96.7 0.8 reshape.208
  97.5 0.7 copy.68
  98.2 0.8 reshape.206
  99.0 0.0 copy-start
  99.0 2.5 %convert_bitcast_fusion = (bf16[1,2,1,4,256,256]{5,4,3,1,2,0:T(8,128)(2,1)}, f32[4,256,256]{2,1,0:T(8,128)}) fusion(bf16[2,256,4,256]{1,3,2,0:T(8,128)(2,1)S(1)} %copy.68, bf16[2,256,4,256]{3,2,1,0:T(4,128)(2,1)S(1)} %reshape.206), kind=kOutput, calls=%fused_computation.30 | convolution fusion | flops 269221888 | bytes 4194304 | tf_op jit(solution)/shard_map/cjhe,cjhf->chef/dot_general | solution.py:283
  101.5 0.0 copy-done
  101.5 1.6 copy.70
  103.1 0.9 convert_element_type.246
  104.0 1.9 collective-permute-start
  105.8 1.9 reshape.207
  107.7 0.0 slice-start.1
  107.7 0.0 copy-start.3
  107.7 0.0 copy-start.4
  107.7 2.7 %reshape_reshape.3 = bf16[1,2,1,256,4,256]{5,4,3,1,2,0:T(4,128)(2,1)} reshape(bf16[512,1024]{1,0:T(8,128)(2,1)} %get-tuple-element.19) | data formatting | bytes 2097152 | tf_op jit(solution)/shard_map/reshape;reshape | solution.py:290
  110.5 0.0 slice-done.1
  110.5 0.1 slice.84
  110.5 1.4 copy.65
  111.9 0.1 convert_add_fusion.2
  112.0 0.0 copy-done.3
  112.1 0.0 copy-done.4
  112.1 8.3 %fusion = f32[256,256,4,2]{1,2,3,0:T(4,128)} fusion(f32[9,4,2,256]{0,1,2,3:T(4,128)} %copy.65, f32[9]{0:T(128)S(1)} %copy-done.4, s32[256,256]{1,0:T(8,128)S(1)} %convert_add_fusion.2, pred[256,256]{1,0:T(8,128)(4,1)S(1)} %iota_compare_fusion.1), kind=kOutput, calls=%fused_computation | convolution fusion | flops 58392576 | bytes 2498596 | tf_op jit(solution)/shard_map/lij,lhci->chij/dot_general | solution.py:279
  120.4 0.0 collective-permute-done
  120.4 2.0 %fusion.22 = bf16[4,256,256]{1,2,0:T(8,128)(2,1)} fusion(f32[4,256,256]{1,2,0:T(8,128)S(1)} %copy.70, bf16[4,256,256]{1,2,0:T(8,128)(2,1)} %collective-permute-done), kind=kLoop, calls=%fused_computation.34 | loop fusion | flops 786432 | bytes 2097152 | tf_op jit(solution)/shard_map/convert_element_type | solution.py:301
  122.3 0.5 collective-permute-start.1
  122.8 4.6 %fusion.15 = f32[2,4,256,256]{3,2,1,0:T(8,128)} fusion(f32[256,256,4,2]{1,2,3,0:T(4,128)} %fusion, bf16[2,256,4,256]{1,3,2,0:T(8,128)(2,1)S(1)} %copy.68, bf16[2,256,4,256]{3,2,1,0:T(4,128)(2,1)} %copy-done, bf16[2,256,4,256]{3,2,1,0:T(4,128)(2,1)S(1)} %reshape.207), kind=kOutput, calls=%fused_computation.21 | convolution fusion | flops 537919488 | bytes 7340032 | tf_op jit(solution)/shard_map/chij,cjhe->cihe/dot_general | solution.py:282
  127.4 9.1 %collective-permute-done.1 = bf16[4,256,256]{1,2,0:T(8,128)(2,1)} collective-permute-done((bf16[4,256,256]{1,2,0:T(8,128)(2,1)}, bf16[4,256,256]{1,2,0:T(8,128)(2,1)}, u32[]{:S(2)}, u32[]{:S(2)}) %collective-permute-start.1) | collective-permute-done | bytes 524320 | tf_op jit(solution)/shard_map/ppermute | solution.py:241
  136.5 1.4 fusion.35
  137.8 0.0 slice-start
  137.8 0.0 copy-start.2
  137.8 0.1 collective-permute-start.2
  137.9 1.6 bitcast_multiply_fusion.3
  139.6 0.0 slice-done
  139.6 0.0 copy-done.2
  139.6 0.5 fusion.18
  140.1 10.8 %collective-permute-done.2 = bf16[4,256,256]{1,2,0:T(8,128)(2,1)S(1)} collective-permute-done((bf16[4,256,256]{1,2,0:T(8,128)(2,1)S(1)}, bf16[4,256,256]{1,2,0:T(8,128)(2,1)S(1)}, u32[]{:S(2)}, u32[]{:S(2)}) %collective-permute-start.2) | collective-permute-done | bytes 524320 | tf_op jit(solution)/shard_map/ppermute | solution.py:241
  150.9 1.5 add_convert_fusion
  152.4 2.2 %collective-permute-start.3 = (bf16[4,256,256]{1,2,0:T(8,128)(2,1)S(1)}, bf16[4,256,256]{1,2,0:T(8,128)(2,1)S(1)}, u32[]{:S(2)}, u32[]{:S(2)}) collective-permute-start(bf16[4,256,256]{1,2,0:T(8,128)(2,1)S(1)} %add_convert_fusion), channel_id=1, source_target_pairs={{0,8},{1,9},{2,10},{3,11},{4,12},{5,13},{6,14},{7,15},{8,0},{9,1},... | collective-permute-start | bytes 1572872 | tf_op jit(solution)/shard_map/ppermute | solution.py:241
  154.5 1.5 fusion.26
  156.0 0.0 copy-start.1
  156.0 0.5 fusion.24
  156.5 20.2 %collective-permute-done.3 = bf16[4,256,256]{1,2,0:T(8,128)(2,1)S(1)} collective-permute-done((bf16[4,256,256]{1,2,0:T(8,128)(2,1)S(1)}, bf16[4,256,256]{1,2,0:T(8,128)(2,1)S(1)}, u32[]{:S(2)}, u32[]{:S(2)}) %collective-permute-start.3) | collective-permute-done | bytes 524320 | tf_op jit(solution)/shard_map/ppermute | solution.py:241
  176.7 0.0 copy-done.1
  176.7 0.8 fusion.7
  177.5 0.7 copy.83
  178.2 0.2 copy.87
  178.4 0.0 all-gather.2.cloned.1.call-done
  178.5 5.8 %convolution_convert_fusion = bf16[512,2048]{1,0:T(8,128)(2,1)} fusion(bf16[512,1024]{1,0:T(8,128)(2,1)S(1)} %bitcast.99, bf16[1024,2048]{1,0:T(8,128)(2,1)} %all-gather.2.cloned.1.call-done), kind=kOutput, calls=%fused_computation.5 | convolution fusion | flops 2148532224 | bytes 7340032 | tf_op jit(solution)/shard_map/dot_general | solution.py:311
  (3 shorter events, 0.0 us)
Async XLA Ops:
  6.5 171.9 %all-gather.2.cloned.1.call-start = ((), (), s32[]{:S(2)}) async-start(), calls=%async_computation | async-start | bytes 4456448 | tf_op jit(solution)/shard_map/all_gather | solution.py:313
  99.0 2.5 %copy-start = (bf16[2,256,4,256]{3,2,1,0:T(4,128)(2,1)}, bf16[2,256,4,256]{3,2,1,0:T(4,128)(2,1)S(1)}, u32[]{:S(2)}) copy-start(bf16[2,256,4,256]{3,2,1,0:T(4,128)(2,1)S(1)} %reshape.206) | copy-start | bytes 3145732
  104.0 16.4 %collective-permute-start = (bf16[4,256,256]{1,2,0:T(8,128)(2,1)}, bf16[4,256,256]{1,2,0:T(8,128)(2,1)}, u32[]{:S(2)}, u32[]{:S(2)}) collective-permute-start(bf16[4,256,256]{1,2,0:T(8,128)(2,1)} %convert_element_type.246), channel_id=1, source_target_pairs={{0,1},{1,0},{2,3},{3,2},{4,5},{5,4},{6,7},{7,6},{8,9},{9,8},{10,11... | collective-permute-start | bytes 1572872 | tf_op jit(solution)/shard_map/ppermute | solution.py:241
  107.7 2.8 %slice-start.1 = ((f32[14,4,512]{2,1,0:T(4,128)}), f32[9,4,512]{2,1,0:T(4,128)S(1)}, s32[]{:S(2)}) async-start(f32[14,4,512]{2,1,0:T(4,128)} %param.10), calls=%async_computation.2 | async-start | bytes 147456 | tf_op jit(solution)/shard_map/slice | solution.py:279
  107.7 4.3 %copy-start.3 = (f32[14,4,512]{2,1,0:T(4,128)S(1)}, f32[14,4,512]{2,1,0:T(4,128)}, u32[]{:S(2)}) copy-start(f32[14,4,512]{2,1,0:T(4,128)} %param.10) | copy-start | bytes 344068
  107.7 4.3 %copy-start.4 = (f32[9]{0:T(128)S(1)}, f32[9]{0:T(128)}, u32[]{:S(2)}) copy-start(f32[9]{0:T(128)} %constant.101.clone) | copy-start | bytes 112
  122.3 14.1 %collective-permute-start.1 = (bf16[4,256,256]{1,2,0:T(8,128)(2,1)}, bf16[4,256,256]{1,2,0:T(8,128)(2,1)}, u32[]{:S(2)}, u32[]{:S(2)}) collective-permute-start(bf16[4,256,256]{1,2,0:T(8,128)(2,1)} %fusion.22), channel_id=1, source_target_pairs={{0,2},{1,3},{2,0},{3,1},{4,6},{5,7},{6,4},{7,5},{8,10},{9,11},{10,... | collective-permute-start | bytes 1572872 | tf_op jit(solution)/shard_map/ppermute | solution.py:241
  137.8 1.7 slice-start
  137.8 1.7 copy-start.2
  137.8 13.0 %collective-permute-start.2 = (bf16[4,256,256]{1,2,0:T(8,128)(2,1)S(1)}, bf16[4,256,256]{1,2,0:T(8,128)(2,1)S(1)}, u32[]{:S(2)}, u32[]{:S(2)}) collective-permute-start(bf16[4,256,256]{1,2,0:T(8,128)(2,1)S(1)} %fusion.35), channel_id=1, source_target_pairs={{0,4},{1,5},{2,6},{3,7},{4,0},{5,1},{6,2},{7,3},{8,12},{9,13},{10,... | collective-permute-start | bytes 1572872 | tf_op jit(solution)/shard_map/ppermute | solution.py:241
  152.4 24.3 %collective-permute-start.3 = (bf16[4,256,256]{1,2,0:T(8,128)(2,1)S(1)}, bf16[4,256,256]{1,2,0:T(8,128)(2,1)S(1)}, u32[]{:S(2)}, u32[]{:S(2)}) collective-permute-start(bf16[4,256,256]{1,2,0:T(8,128)(2,1)S(1)} %add_convert_fusion), channel_id=1, source_target_pairs={{0,8},{1,9},{2,10},{3,11},{4,12},{5,13},{6,14},{7,15},{8,0},{9,1},... | collective-permute-start | bytes 1572872 | tf_op jit(solution)/shard_map/ppermute | solution.py:241
  156.0 20.6 %copy-start.1 = (f32[2,4,256,256]{3,2,1,0:T(8,128)S(1)}, f32[2,4,256,256]{3,2,1,0:T(8,128)}, u32[]{:S(2)}) copy-start(f32[2,4,256,256]{3,2,1,0:T(8,128)} %fusion.15) | copy-start | bytes 6291460
Sparse Core Ops, SparseCore 0:
  9.5 67.3 all-gather.1

commit v2 on v1

v2 whole, which is shorter than its diff:
```python
import functools
import math

import jax
import jax.numpy as jnp
from jax import lax
from jax.experimental import pallas as pl
from jax.experimental.pallas import tpu as pltpu
from jax.sharding import PartitionSpec as P

HEADS = 4
HEAD = 256
SPAN = 256
CBITS = 8
MESH = pl.DeviceIdType.MESH


class Place:
    def __init__(self, groups, seqs):
        self.seqs = seqs
        self.chips = seqs // 2
        self.has_x = groups % 2 == 0
        self.g = lax.axis_index("group")
        self.me = lax.axis_index("seq")
        self.core = lax.rem(self.me, 2)
        self.chip = self.me // 2
        odd = lax.rem(self.chip, 2)
        half = self.chip // 2
        self.pos = half + odd * (self.chips - 1 - 2 * half)
        self.par = lax.rem(self.g, 2)
        self.mate = (self.g, self.me + 1 - 2 * self.core)
        self.cross = (self.g + 1 - 2 * self.par, self.me)

    def chip_at(self, offset):
        pos = lax.rem(self.pos + offset + self.chips, self.chips)
        late = pos // (self.chips // 2)
        return 2 * pos + late * (2 * (self.chips - 1) + 1 - 4 * pos)

    def ring(self, offset):
        return (self.g, self.chip_at(offset) * 2 + self.core)

    def flip(self, bit):
        return (self.g, self.me + (1 - 2 * self.digit(bit)) * 2**bit)

    def digit(self, bit):
        return lax.rem(self.me // 2**bit, 2)

    def greet(self, others):
        barrier = pltpu.get_barrier_semaphore()
        for other in others:
            pl.semaphore_signal(barrier, inc=1, device_id=other, device_id_type=MESH)
        pl.semaphore_wait(barrier, len(others))

    def neighbours(self):
        found = [self.ring(1), self.ring(-1), self.mate]
        return found + [self.cross] if self.has_x else found


def relay_columns(columns, has_x, share):
    return (columns // share) // 128 * 128 if has_x else 0


class Gather:
    def __init__(self, place, buf, send_sem, recv_sem, share):
        self.at = place
        self.buf = buf
        self.send_sem, self.recv_sem = send_sem, recv_sem
        _, self.rows, self.columns = buf.shape
        self.sub = 2 if self.rows % 32 == 0 else 1
        self.part = self.rows // self.sub
        self.rel = relay_columns(self.columns, place.has_x, share)
        self.slots, self.sent = {}, []
        keep = self.columns - self.rel
        self.ring_cols = (place.par * self.rel, keep) if self.rel else (0, keep)
        self.give_cols = (place.par * keep, self.rel)
        self.take_cols = ((1 - place.par) * keep, self.rel)
        self.last = place.chips // 2

    def view(self, index, h, cols):
        start, width = cols
        if not isinstance(start, int):
            start = pl.multiple_of(start, 128)
        return self.buf.at[index, pl.ds(h * self.part, self.part), pl.ds(start, width)]

    def copy(self, key, index, h, cols, device):
        slot = self.slots.setdefault(key, len(self.slots))
        ref = self.view(index, h, cols)
        return pltpu.make_async_remote_copy(
            src_ref=ref,
            dst_ref=ref,
            send_sem=self.send_sem.at[slot],
            recv_sem=self.recv_sem.at[slot],
            device_id=device,
            device_id_type=MESH,
        )

    def send(self, *args):
        one = self.copy(*args)
        one.start()
        self.sent.append(one)

    def mine(self, offset):
        return self.at.chip_at(offset) * 2 + self.at.core

    def theirs(self, offset):
        return self.at.chip_at(offset) * 2 + 1 - self.at.core

    def pieces(self, step):
        every = [(h, d) for h in range(self.sub) for d in (1, -1)]
        if step < self.last:
            return every
        return [(0, 1), (1, -1)] if self.sub == 2 else [(0, 1)]

    def begin(self):
        for h, d in self.pieces(1):
            self.send(("ring", 1, h, d), self.at.me, h, self.ring_cols, self.at.ring(d))
        for h in range(self.sub):
            self.send(("own", h), self.at.me, h, (0, self.columns), self.at.mate)

    def own(self):
        for h in range(self.sub):
            self.copy(("own", h), self.theirs(0), h, (0, self.columns), self.at.mate).wait_recv()

    def arrive(self, step):
        for h, d in self.pieces(step):
            index = self.mine(-d * step)
            self.copy(("ring", step, h, d), index, h, self.ring_cols, self.at.ring(-d)).wait_recv()
            if step < self.last and (h, d) in self.pieces(step + 1):
                self.send(("ring", step + 1, h, d), index, h, self.ring_cols, self.at.ring(d))
            if step < self.last and self.rel:
                self.send(("cross", step, h, d), index, h, self.give_cols, self.at.cross)
            self.send(("mate", step, h, d), index, h, self.ring_cols, self.at.mate)

    def complete(self, step):
        if self.rel:
            for h, d in self.pieces(step):
                index = self.mine(-d * step)
                if step < self.last:
                    self.copy(("cross", step, h, d), index, h, self.take_cols, self.at.cross).wait_recv()
                    if step + 1 == self.last and (h, d) in self.pieces(step + 1):
                        self.send(("end", h, d), index, h, self.take_cols, self.at.ring(d))
                else:
                    self.copy(("end", h, d), index, h, self.take_cols, self.at.ring(-d)).wait_recv()
                self.send(("pass", step, h, d), index, h, self.take_cols, self.at.mate)
        for h, d in self.pieces(step):
            index = self.theirs(-d * step)
            self.copy(("mate", step, h, d), index, h, self.ring_cols, self.at.mate).wait_recv()
            if self.rel:
                self.copy(("pass", step, h, d), index, h, self.take_cols, self.at.mate).wait_recv()
        return (step, -step) if step < self.last else (step,)

    def run(self, use, before_end):
        self.own()
        use(self.at.chip_at(0))
        for step in range(1, self.last):
            self.arrive(step)
            if step > 1:
                for offset in self.complete(step - 1):
                    use(self.at.chip_at(offset))
        for offset in self.complete(self.last - 1):
            use(self.at.chip_at(offset))
        self.arrive(self.last)
        before_end()
        for offset in self.complete(self.last):
            use(self.at.chip_at(offset))

    def drain(self):
        for one in self.sent:
            one.wait_send()


def slots_needed(seqs):
    return 4 * seqs + 8


class Exchange:
    def __init__(self, place, left, send_sem, recv_sem):
        self.at, self.left = place, left
        self.send_sem, self.recv_sem = send_sem, recv_sem
        self.slots, self.sent = {}, []
        self.c, self.y = place.core, place.digit(1)
        self.head = 2 * self.c + self.y
        self.other = 2 * self.c + 1 - self.y
        self.mate_head = 2 * (1 - self.c) + self.y
        self.mate_other = 2 * (1 - self.c) + 1 - self.y

    def copy(self, key, src, bit, head, device):
        slot = self.slots.setdefault(key, len(self.slots))
        return pltpu.make_async_remote_copy(
            src_ref=src,
            dst_ref=self.left.at[bit, head],
            send_sem=self.send_sem.at[slot],
            recv_sem=self.recv_sem.at[slot],
            device_id=device,
            device_id_type=MESH,
        )

    def send(self, *args):
        one = self.copy(*args)
        one.start()
        self.sent.append(one)

    def forward(self, key, bit, head, device):
        self.send(key, self.left.at[bit, head], bit, head, device)

    def wait(self, key, bit, head, device):
        self.copy(key, self.left.at[bit, head], bit, head, device).wait_recv()

    def spread(self, bit):
        self.forward(("quad", bit), bit, self.head, self.at.flip(1))
        self.forward(("near", bit), bit, self.head, self.at.mate)

    def collect(self, bit):
        if bit > 1:
            self.wait(("quad", bit), bit, self.other, self.at.flip(1))
        else:
            self.wait(("across", 1), bit, self.other, self.at.flip(1))
        self.forward(("far", bit), bit, self.other, self.at.mate)
        self.wait(("near", bit), bit, self.mate_head, self.at.mate)
        self.wait(("far", bit), bit, self.mate_other, self.at.mate)

    def drain(self):
        for one in self.sent:
            one.wait_send()


def product(a, b, dims):
    return lax.dot_general(a, b, (dims, ((), ())), preferred_element_type=jnp.float32)


def head_cols(h):
    return pl.ds(h * HEAD, HEAD)


def layer_kernel(
    groups, seqs, tokens_ref, w_ref, wo_ref, weight_ref, out_ref,
    buf, total, qkv, wo_buf, mix, acc, attended, local_sum, first_sum, give, pair, pair_give, run_give, left,
    load_sem, send_sem, recv_sem, wo_send, wo_recv, ex_send, ex_recv,
):
    place = Place(groups, seqs)
    load = pltpu.make_async_copy(w_ref, buf.at[place.me], load_sem.at[0])
    load.start()
    load_o = pltpu.make_async_copy(wo_ref, wo_buf.at[place.me], load_sem.at[1])
    load_o.start()
    seq_bits = seqs.bit_length() - 1
    place.greet(place.neighbours() + [place.flip(b) for b in range(1, seq_bits)])
    load.wait()
    gather = Gather(place, buf, send_sem, recv_sem, 3)
    gather.begin()
    load_o.wait()
    gather_o = Gather(place, wo_buf, wo_send, wo_recv, 3)

    count = tokens_ref.shape[0] // SPAN
    wide = HEADS * HEAD

    @pl.loop(0, count)
    def _(c):
        rows = pl.ds(pl.multiple_of(c * SPAN, SPAN), SPAN)
        i = lax.broadcasted_iota(jnp.int32, (SPAN, SPAN), 0)
        j = lax.broadcasted_iota(jnp.int32, (SPAN, SPAN), 1)
        apart = i ^ j
        for h in range(HEADS):
            value = jnp.zeros((SPAN, SPAN), jnp.float32)
            for level in range(CBITS + 1):
                gain = 1.0 / math.sqrt(HEAD * max(1, 2 ** (level - 1)))
                column = weight_ref[rows, level * HEADS + h : level * HEADS + h + 1] * gain
                column = jnp.broadcast_to(column, (SPAN, SPAN))
                value = column if level == 0 else jnp.where(apart >= 2 ** (level - 1), column, value)
            mix[c, h] = jnp.where(i >= j, value, 0.0)

    rows_w, columns = w_ref.shape
    tile = 512
    aligned = (2 * rows_w) % 128 == 0
    started = []

    def use(chip):
        if not aligned:
            return
        started.append(1)
        step = len(started)
        x = tokens_ref[:, pl.ds(pl.multiple_of(chip * (2 * rows_w), 128), 2 * rows_w)]

        @pl.loop(0, columns // tile)
        def _(t):
            cols = pl.ds(pl.multiple_of(t * tile, tile), tile)
            w = buf[pl.ds(chip * 2, 2), :, cols].reshape(2 * rows_w, tile)
            y = jnp.dot(x, w, preferred_element_type=jnp.float32)
            if step == 1:
                total[:, cols] = y
            elif step == place.chips:
                qkv[:, cols] = (total[:, cols] + y).astype(qkv.dtype)
            else:
                total[:, cols] += y

    gather.run(use, gather_o.begin)
    if not aligned:

        @pl.loop(0, columns // tile)
        def _(t):
            cols = pl.ds(pl.multiple_of(t * tile, tile), tile)
            w = buf[:, :, cols].reshape(seqs * rows_w, tile)
            y = jnp.dot(tokens_ref[...], w, preferred_element_type=jnp.float32)
            qkv[:, cols] = y.astype(qkv.dtype)

    for h in range(HEADS):
        for c in range(count):
            k = qkv[pl.ds(c * SPAN, SPAN), head_cols(HEADS + h)]
            v = qkv[pl.ds(c * SPAN, SPAN), head_cols(2 * HEADS + h)]
            state = product(k, v, ((0,), (0,)))
            if c == 0:
                local_sum[h] = state
                first_sum[h] = state.astype(jnp.bfloat16)
            else:
                local_sum[h] += state
        give[h] = local_sum[h].astype(jnp.bfloat16)
    exchange = Exchange(place, left, ex_send, ex_recv)
    for h in range(HEADS):
        exchange.send(("core", h), give.at[h], 0, h, place.mate)

    def attend(c):
        rows = pl.ds(c * SPAN, SPAN)
        for h in range(HEADS):
            q = qkv[rows, head_cols(h)]
            k = qkv[rows, head_cols(HEADS + h)]
            v = qkv[rows, head_cols(2 * HEADS + h)]
            scores = product(q, k, ((1,), (1,)))
            probs = (scores * mix[c, h]).astype(jnp.bfloat16)
            acc[rows, head_cols(h)] = product(probs, v, ((1,), (0,)))

    def gain_of(level):
        return 1.0 / math.sqrt(SPAN * 2 ** (level - 1) * HEAD)

    def weight_of(rows, level, h):
        at = (CBITS + level) * HEADS + h
        return weight_ref[rows, at : at + 1]

    def read(bit):
        level = local_bits + bit + 1
        scale = place.digit(bit).astype(jnp.float32) * gain_of(level)
        every = pl.ds(0, count * SPAN)
        for h in range(HEADS):
            got = product(qkv[:, head_cols(h)], left[bit, h], ((1,), (0,)))
            acc[:, head_cols(h)] += got * (weight_of(every, level, h) * scale)

    local_bits = count.bit_length() - 1
    attend(0)
    gather_o.own()
    gather_o.arrive(1)
    for h in range(HEADS):
        exchange.wait(("core", h), 0, h, place.mate)
    for n in range(2):
        h = 2 * place.core + n
        pair[n] = local_sum[h] + left[0, h].astype(jnp.float32)
        pair_give[n] = pair[n].astype(jnp.bfloat16)
    y = place.digit(1)
    for n, which in enumerate((1 - y, y)):
        exchange.send(("across", n), pair_give.at[which], 1, 2 * place.core + which, place.flip(1))
    for c in range(1, count):
        attend(c)
    for c in range(1, count):
        rows = pl.ds(c * SPAN, SPAN)
        for h in range(HEADS):
            got = product(qkv[rows, head_cols(h)], first_sum[h], ((1,), (0,)))
            acc[rows, head_cols(h)] += got * (weight_of(rows, 1, h) * gain_of(1))
    steps = iter(range(2, gather_o.last + 1))
    done_o = [1]

    def advance():
        step = next(steps, None)
        if step is not None:
            if step == gather_o.last:
                gather_o.complete(step - 1)
                gather_o.arrive(step)
            else:
                gather_o.arrive(step)
                gather_o.complete(step - 1)
            done_o.append(step)

    exchange.wait(("across", 0), 1, exchange.head, place.flip(1))
    running = pair[y] + left[1, exchange.head].astype(jnp.float32)
    exchange.forward(("near", 1), 1, exchange.head, place.mate)
    for bit in range(2, seq_bits):
        run_give[bit] = running.astype(jnp.bfloat16)
        exchange.send(("hop", bit), run_give.at[bit], bit, exchange.head, place.flip(bit))
        exchange.collect(bit - 1)
        advance()
        read(bit - 2)
        exchange.wait(("hop", bit), bit, exchange.head, place.flip(bit))
        exchange.spread(bit)
        if bit + 1 < seq_bits:
            running = running + left[bit, exchange.head].astype(jnp.float32)
    read(seq_bits - 2)
    while done_o[-1] < gather_o.last:
        advance()
    exchange.collect(seq_bits - 1)
    gather_o.complete(gather_o.last)
    read(seq_bits - 1)

    attended[...] = acc[...].astype(jnp.bfloat16)

    @pl.loop(0, wo_ref.shape[1] // tile)
    def _(t):
        cols = pl.ds(pl.multiple_of(t * tile, tile), tile)
        w = wo_buf[:, :, cols].reshape(wide, tile)
        out_ref[:, cols] = jnp.dot(
            attended[...], w, preferred_element_type=jnp.float32
        ).astype(out_ref.dtype)

    gather.drain()
    gather_o.drain()
    exchange.drain()


def on_device(tokens, w_qkv, w_out, level_weight):
    groups, seqs = lax.axis_size("group"), lax.axis_size("seq")
    rows = tokens.shape[0]
    count = rows // SPAN
    seq_bits = seqs.bit_length() - 1
    weights = level_weight.reshape(-1, rows).T
    square = (HEAD, HEAD)
    vmem = pl.BlockSpec(memory_space=pltpu.VMEM)
    hbm = pl.BlockSpec(memory_space=pl.ANY)
    sems = pltpu.SemaphoreType.DMA((slots_needed(seqs),))
    return pl.pallas_call(
        functools.partial(layer_kernel, groups, seqs),
        out_shape=jax.ShapeDtypeStruct((rows, w_out.shape[1]), jnp.bfloat16),
        in_specs=[vmem, hbm, hbm, vmem],
        out_specs=vmem,
        scratch_shapes=[
            pltpu.VMEM((seqs, *w_qkv.shape), jnp.bfloat16),
            pltpu.VMEM((rows, w_qkv.shape[1]), jnp.float32),
            pltpu.VMEM((rows, w_qkv.shape[1]), jnp.bfloat16),
            pltpu.VMEM((seqs, *w_out.shape), jnp.bfloat16),
            pltpu.VMEM((count, HEADS, SPAN, SPAN), jnp.float32),
            pltpu.VMEM((rows, HEADS * HEAD), jnp.float32),
            pltpu.VMEM((rows, HEADS * HEAD), jnp.bfloat16),
            pltpu.VMEM((HEADS, *square), jnp.float32),
            pltpu.VMEM((HEADS, *square), jnp.bfloat16),
            pltpu.VMEM((HEADS, *square), jnp.bfloat16),
            pltpu.VMEM((2, *square), jnp.float32),
            pltpu.VMEM((2, *square), jnp.bfloat16),
            pltpu.VMEM((seq_bits, *square), jnp.bfloat16),
            pltpu.VMEM((seq_bits, HEADS, *square), jnp.bfloat16),
            pltpu.SemaphoreType.DMA((2,)),
            sems, sems, sems, sems,
            pltpu.SemaphoreType.DMA((8 * seq_bits,)),
            pltpu.SemaphoreType.DMA((8 * seq_bits,)),
        ],
        compiler_params=pltpu.CompilerParams(
            collective_id=0, has_side_effects=True, vmem_limit_bytes=63 * 1024 * 1024
        ),
    )(tokens, w_qkv, w_out, weights)


def solution(mesh):
    return jax.shard_map(
        on_device,
        mesh=mesh,
        in_specs=(
            P(("group", "seq"), None),
            P("seq", None),
            P("seq", None),
            P(None, None, ("group", "seq")),
        ),
        out_specs=P(("group", "seq"), None),
        check_vma=False,
    )
```

time: 192 us -> 106 us (0.55)
  waiting for transfers between devices: 40.8 us -> 0 us
  matrix products: 26.1 us -> 0 us
  Pallas kernels: 86.2 us -> 101 us
  between operations: 13.6 us -> 0.01 us
  local copies, waits for them, and re-layouts: 14 us -> 4.93 us
  other arithmetic: 5.81 us -> 0 us
  starting transfers between devices: 4.56 us -> 0 us
    ppermute x4 -> x0, waiting for transfers between devices: 40.1 us -> none  [partner_2(): return lax.ppermute(value, axis, pairs)]
    dot_general x9 -> x0, matrix products: 26.1 us -> none  [the longest x1 8.28 us: on_device(): jnp.einsum('lij,lhci->chij', table, weights[:CBITS + 1], precision=highest)]
    pallas_call x1, Pallas kernels: 86.2 us -> 101 us  [on_device(): pl.pallas_call(functools.partial(layer_kernel, groups, seqs), out_shape=j...]
    convert_element_type x4 -> x0, other arithmetic: 5.67 us -> none  [on_device(): partner = partner_2(block_total.astype(jnp.bfloat16), 'seq', bit_pos)]
    slice x7 -> x0, local copies, waits for them, and re-layouts: 4.68 us -> none  [the longest x1 3.23 us: on_device(): value_rows = qkv[:, 2 * head_cols:].reshape(count, SPAN, HEADS, HEAD)]
    ppermute x4 -> x0, starting transfers between devices: 4.56 us -> none  [partner_2(): return lax.ppermute(value, axis, pairs)]
    unnamed x11 -> x1, local copies, waits for them, and re-layouts: 0.24 us -> 3.16 us
    another operation x1 -> x0, local copies, waits for them, and re-layouts: 2.72 us -> none  [on_device(): right_q = queries.reshape(blocks, 2, half_size, SPAN, HEADS, HEAD)[:, 1]]
  transfers between devices with their start and end apart: 5 -> 0, of which waited for: 3 -> 0; matrix products, arithmetic and copies ran while one was open for 21% -> 0% of each run, Pallas kernels for 45% -> 0%
where the time goes in v2:
time: 106 us
  Pallas kernels  101 us (95%)
  local copies, waits for them, and re-layouts  4.93 us (5%)
    pallas_call x1, Pallas kernels, on_device(): pl.pallas_call(functools.partial(layer_kernel, groups, seqs), out_shape=j...  101 us
    unnamed x1, local copies, waits for them, and re-layouts  3.16 us

profile of v2, /device:TPU:0, one launch (start us, length us, event | category | flops | bytes accessed | tf_op | source)
XLA Modules:
  0.0 105.9 jit_solution(12064320457991187134)
XLA Ops:
  0.0 0.9 reshape.3
  0.9 0.8 copy.6
  1.8 100.9 %shard_map.46 = bf16[512,2048]{1,0:T(8,128)(2,1)} custom-call(bf16[512,2048]{1,0:T(8,128)(2,1)} %tokens_ref.1, bf16[128,3072]{1,0:T(8,128)(2,1)} %w_ref.1, bf16[64,2048]{1,0:T(8,128)(2,1)} %wo_ref.1, f32[512,56]{1,0:T(8,128)} %bitcast.1), custom_call_target="tpu_custom_call" | custom-call | tf_op jit(solution)/shard_map/pallas_call | solution.py:424
  102.7 3.2 %copy.8 = bf16[512,2048]{1,0:T(8,128)(2,1)} copy(bf16[512,2048]{1,0:T(8,128)(2,1)} %shard_map.46) | data formatting | bytes 4194304

commit v3 on v2

--- a/solution.py
+++ b/solution.py
@@ -149,7 +149,7 @@
                 self.copy(("pass", step, h, d), index, h, self.take_cols, self.at.mate).wait_recv()
         return (step, -step) if step < self.last else (step,)
 
-    def run(self, use, before_end):
+    def steps(self, use, before_end):
         self.own()
         use(self.at.chip_at(0))
         for step in range(1, self.last):
@@ -157,10 +157,12 @@
             if step > 1:
                 for offset in self.complete(step - 1):
                     use(self.at.chip_at(offset))
+            yield
         for offset in self.complete(self.last - 1):
             use(self.at.chip_at(offset))
         self.arrive(self.last)
         before_end()
+        yield
         for offset in self.complete(self.last):
             use(self.at.chip_at(offset))
 
@@ -233,25 +235,38 @@
 
 
 def layer_kernel(
-    groups, seqs, tokens_ref, w_ref, wo_ref, weight_ref, out_ref,
-    buf, total, qkv, wo_buf, mix, acc, attended, local_sum, first_sum, give, pair, pair_give, run_give, left,
-    load_sem, send_sem, recv_sem, wo_send, wo_recv, ex_send, ex_recv,
+    groups, seqs, tokens_hbm, w_ref, wo_ref, weight_ref, out_ref,
+    tokens_ref, kv_buf, q_buf, wo_buf, total, qkv, mix, acc, attended, local_sum, first_sum, give, pair, pair_give,
+    run_give, left, load_sem, kv_send, kv_recv, q_send, q_recv, wo_send, wo_recv, ex_send, ex_recv,
 ):
     place = Place(groups, seqs)
-    load = pltpu.make_async_copy(w_ref, buf.at[place.me], load_sem.at[0])
-    load.start()
-    load_o = pltpu.make_async_copy(wo_ref, wo_buf.at[place.me], load_sem.at[1])
-    load_o.start()
+    rows_w, columns = w_ref.shape
+    wide = HEADS * HEAD
+    here = place.me
+    loads = [
+        pltpu.make_async_copy(src, dst, load_sem.at[n])
+        for n, (src, dst) in enumerate(
+            (
+                (w_ref.at[:, pl.ds(wide, columns - wide)], kv_buf.at[here]),
+                (w_ref.at[:, pl.ds(0, wide)], q_buf.at[here]),
+                (wo_ref, wo_buf.at[here]),
+                (tokens_hbm, tokens_ref),
+            )
+        )
+    ]
+    for one in loads:
+        one.start()
     seq_bits = seqs.bit_length() - 1
     place.greet(place.neighbours() + [place.flip(b) for b in range(1, seq_bits)])
-    load.wait()
-    gather = Gather(place, buf, send_sem, recv_sem, 3)
-    gather.begin()
-    load_o.wait()
+    loads[0].wait()
+    gather_kv = Gather(place, kv_buf, kv_send, kv_recv, 3)
+    gather_kv.begin()
+    for one in loads[1:]:
+        one.wait()
+    gather_q = Gather(place, q_buf, q_send, q_recv, 3)
     gather_o = Gather(place, wo_buf, wo_send, wo_recv, 3)
 
     count = tokens_ref.shape[0] // SPAN
-    wide = HEADS * HEAD
 
     @pl.loop(0, count)
     def _(c):
@@ -268,39 +283,47 @@
                 value = column if level == 0 else jnp.where(apart >= 2 ** (level - 1), column, value)
             mix[c, h] = jnp.where(i >= j, value, 0.0)
 
-    rows_w, columns = w_ref.shape
     tile = 512
     aligned = (2 * rows_w) % 128 == 0
-    started = []
-
-    def use(chip):
-        if not aligned:
+
+    def user(buf, base):
+        started = []
+
+        def use(chip):
+            if not aligned:
+                return
+            started.append(1)
+            step = len(started)
+            x = tokens_ref[:, pl.ds(pl.multiple_of(chip * (2 * rows_w), 128), 2 * rows_w)]
+
+            @pl.loop(0, buf.shape[2] // tile)
+            def _(t):
+                cols = pl.ds(pl.multiple_of(t * tile, tile), tile)
+                w = buf[pl.ds(chip * 2, 2), :, cols].reshape(2 * rows_w, tile)
+                y = jnp.dot(x, w, preferred_element_type=jnp.float32)
+                if step == 1:
+                    total[:, cols] = y
+                elif step == place.chips:
+                    qkv[:, pl.ds(pl.multiple_of(base + t * tile, tile), tile)] = (total[:, cols] + y).astype(qkv.dtype)
+                else:
+                    total[:, cols] += y
+
+        return use
+
+    def at_once(buf, base):
+        if aligned:
             return
-        started.append(1)
-        step = len(started)
-        x = tokens_ref[:, pl.ds(pl.multiple_of(chip * (2 * rows_w), 128), 2 * rows_w)]
-
-        @pl.loop(0, columns // tile)
-        def _(t):
-            cols = pl.ds(pl.multiple_of(t * tile, tile), tile)
-            w = buf[pl.ds(chip * 2, 2), :, cols].reshape(2 * rows_w, tile)
-            y = jnp.dot(x, w, preferred_element_type=jnp.float32)
-            if step == 1:
-                total[:, cols] = y
-            elif step == place.chips:
-                qkv[:, cols] = (total[:, cols] + y).astype(qkv.dtype)
-            else:
-                total[:, cols] += y
-
-    gather.run(use, gather_o.begin)
-    if not aligned:
-
-        @pl.loop(0, columns // tile)
+
+        @pl.loop(0, buf.shape[2] // tile)
         def _(t):
             cols = pl.ds(pl.multiple_of(t * tile, tile), tile)
             w = buf[:, :, cols].reshape(seqs * rows_w, tile)
             y = jnp.dot(tokens_ref[...], w, preferred_element_type=jnp.float32)
-            qkv[:, cols] = y.astype(qkv.dtype)
+            qkv[:, pl.ds(pl.multiple_of(base + t * tile, tile), tile)] = y.astype(qkv.dtype)
+
+    for _ in gather_kv.steps(user(kv_buf, wide), gather_q.begin):
+        pass
+    at_once(kv_buf, wide)
 
     for h in range(HEADS):
         for c in range(count):
@@ -317,6 +340,48 @@
     for h in range(HEADS):
         exchange.send(("core", h), give.at[h], 0, h, place.mate)
 
+    def exchange_steps():
+        for h in range(HEADS):
+            exchange.wait(("core", h), 0, h, place.mate)
+        for n in range(2):
+            h = 2 * place.core + n
+            pair[n] = local_sum[h] + left[0, h].astype(jnp.float32)
+            pair_give[n] = pair[n].astype(jnp.bfloat16)
+        y = place.digit(1)
+        for n, which in enumerate((1 - y, y)):
+            exchange.send(("across", n), pair_give.at[which], 1, 2 * place.core + which, place.flip(1))
+        yield
+        exchange.wait(("across", 0), 1, exchange.head, place.flip(1))
+        running = pair[y] + left[1, exchange.head].astype(jnp.float32)
+        run_give[2] = running.astype(jnp.bfloat16)
+        exchange.send(("hop", 2), run_give.at[2], 2, exchange.head, place.flip(2))
+        exchange.forward(("near", 1), 1, exchange.head, place.mate)
+        yield
+        for bit in range(2, seq_bits):
+            exchange.wait(("hop", bit), bit, exchange.head, place.flip(bit))
+            if bit + 1 < seq_bits:
+                running = running + left[bit, exchange.head].astype(jnp.float32)
+                run_give[bit + 1] = running.astype(jnp.bfloat16)
+                exchange.send(("hop", bit + 1), run_give.at[bit + 1], bit + 1, exchange.head, place.flip(bit + 1))
+            exchange.spread(bit)
+            exchange.collect(bit - 1)
+            yield
+        exchange.collect(seq_bits - 1)
+
+    stages = exchange_steps()
+    for _ in gather_q.steps(user(q_buf, 0), gather_o.begin):
+        next(stages, None)
+    at_once(q_buf, 0)
+
+    local_bits = count.bit_length() - 1
+
+    def gain_of(level):
+        return 1.0 / math.sqrt(SPAN * 2 ** (level - 1) * HEAD)
+
+    def weight_of(rows, level, h):
+        at = (CBITS + level) * HEADS + h
+        return weight_ref[rows, at : at + 1]
+
     def attend(c):
         rows = pl.ds(c * SPAN, SPAN)
         for h in range(HEADS):
@@ -325,14 +390,10 @@
             v = qkv[rows, head_cols(2 * HEADS + h)]
             scores = product(q, k, ((1,), (1,)))
             probs = (scores * mix[c, h]).astype(jnp.bfloat16)
-            acc[rows, head_cols(h)] = product(probs, v, ((1,), (0,)))
-
-    def gain_of(level):
-        return 1.0 / math.sqrt(SPAN * 2 ** (level - 1) * HEAD)
-
-    def weight_of(rows, level, h):
-        at = (CBITS + level) * HEADS + h
-        return weight_ref[rows, at : at + 1]
+            got = product(probs, v, ((1,), (0,)))
+            if c > 0:
+                got += product(q, first_sum[h], ((1,), (0,))) * (weight_of(rows, 1, h) * gain_of(1))
+            acc[rows, head_cols(h)] = got
 
     def read(bit):
         level = local_bits + bit + 1
@@ -342,59 +403,17 @@
             got = product(qkv[:, head_cols(h)], left[bit, h], ((1,), (0,)))
             acc[:, head_cols(h)] += got * (weight_of(every, level, h) * scale)
 
-    local_bits = count.bit_length() - 1
-    attend(0)
-    gather_o.own()
-    gather_o.arrive(1)
-    for h in range(HEADS):
-        exchange.wait(("core", h), 0, h, place.mate)
-    for n in range(2):
-        h = 2 * place.core + n
-        pair[n] = local_sum[h] + left[0, h].astype(jnp.float32)
-        pair_give[n] = pair[n].astype(jnp.bfloat16)
-    y = place.digit(1)
-    for n, which in enumerate((1 - y, y)):
-        exchange.send(("across", n), pair_give.at[which], 1, 2 * place.core + which, place.flip(1))
-    for c in range(1, count):
-        attend(c)
-    for c in range(1, count):
-        rows = pl.ds(c * SPAN, SPAN)
-        for h in range(HEADS):
-            got = product(qkv[rows, head_cols(h)], first_sum[h], ((1,), (0,)))
-            acc[rows, head_cols(h)] += got * (weight_of(rows, 1, h) * gain_of(1))
-    steps = iter(range(2, gather_o.last + 1))
-    done_o = [1]
-
-    def advance():
-        step = next(steps, None)
-        if step is not None:
-            if step == gather_o.last:
-                gather_o.complete(step - 1)
-                gather_o.arrive(step)
-            else:
-                gather_o.arrive(step)
-                gather_o.complete(step - 1)
-            done_o.append(step)
-
-    exchange.wait(("across", 0), 1, exchange.head, place.flip(1))
-    running = pair[y] + left[1, exchange.head].astype(jnp.float32)
-    exchange.forward(("near", 1), 1, exchange.head, place.mate)
-    for bit in range(2, seq_bits):
-        run_give[bit] = running.astype(jnp.bfloat16)
-        exchange.send(("hop", bit), run_give.at[bit], bit, exchange.head, place.flip(bit))
-        exchange.collect(bit - 1)
-        advance()
-        read(bit - 2)
-        exchange.wait(("hop", bit), bit, exchange.head, place.flip(bit))
-        exchange.spread(bit)
-        if bit + 1 < seq_bits:
-            running = running + left[bit, exchange.head].astype(jnp.float32)
-    read(seq_bits - 2)
-    while done_o[-1] < gather_o.last:
-        advance()
-    exchange.collect(seq_bits - 1)
-    gather_o.complete(gather_o.last)
-    read(seq_bits - 1)
+    work = [functools.partial(attend, c) for c in range(count)]
+    for _ in gather_o.steps(lambda chip: None, lambda: None):
+        if work:
+            work.pop(0)()
+        next(stages, None)
+    for one in work:
+        one()
+    for _ in stages:
+        pass
+    for bit in range(seq_bits):
+        read(bit)
 
     attended[...] = acc[...].astype(jnp.bfloat16)
 
@@ -406,9 +425,8 @@
             attended[...], w, preferred_element_type=jnp.float32
         ).astype(out_ref.dtype)
 
-    gather.drain()
-    gather_o.drain()
-    exchange.drain()
+    for one in (gather_kv, gather_q, gather_o, exchange):
+        one.drain()
 
 
 def on_device(tokens, w_qkv, w_out, level_weight):
@@ -424,13 +442,15 @@
     return pl.pallas_call(
         functools.partial(layer_kernel, groups, seqs),
         out_shape=jax.ShapeDtypeStruct((rows, w_out.shape[1]), jnp.bfloat16),
-        in_specs=[vmem, hbm, hbm, vmem],
+        in_specs=[hbm, hbm, hbm, vmem],
         out_specs=vmem,
         scratch_shapes=[
-            pltpu.VMEM((seqs, *w_qkv.shape), jnp.bfloat16),
-            pltpu.VMEM((rows, w_qkv.shape[1]), jnp.float32),
+            pltpu.VMEM(tokens.shape, jnp.bfloat16),
+            pltpu.VMEM((seqs, w_qkv.shape[0], 2 * HEADS * HEAD), jnp.bfloat16),
+            pltpu.VMEM((seqs, w_qkv.shape[0], HEADS * HEAD), jnp.bfloat16),
+            pltpu.VMEM((seqs, *w_out.shape), jnp.bfloat16),
+            pltpu.VMEM((rows, 2 * HEADS * HEAD), jnp.float32),
             pltpu.VMEM((rows, w_qkv.shape[1]), jnp.bfloat16),
-            pltpu.VMEM((seqs, *w_out.shape), jnp.bfloat16),
             pltpu.VMEM((count, HEADS, SPAN, SPAN), jnp.float32),
             pltpu.VMEM((rows, HEADS * HEAD), jnp.float32),
             pltpu.VMEM((rows, HEADS * HEAD), jnp.bfloat16),
@@ -441,8 +461,8 @@
             pltpu.VMEM((2, *square), jnp.bfloat16),
             pltpu.VMEM((seq_bits, *square), jnp.bfloat16),
             pltpu.VMEM((seq_bits, HEADS, *square), jnp.bfloat16),
-            pltpu.SemaphoreType.DMA((2,)),
-            sems, sems, sems, sems,
+            pltpu.SemaphoreType.DMA((4,)),
+            sems, sems, sems, sems, sems, sems,
             pltpu.SemaphoreType.DMA((8 * seq_bits,)),
             pltpu.SemaphoreType.DMA((8 * seq_bits,)),
         ],

time: 106 us -> 106 us (level)
  no operation moved by 1% of the time
where the time goes in v3:
time: 106 us; the launch traced here: 105 us
  Pallas kernels  100 us (94%)
  local copies, waits for them, and re-layouts  4.93 us (5%)
    pallas_call x1, Pallas kernels, on_device(): pl.pallas_call(functools.partial(layer_kernel, groups, seqs), out_shape=j...  100 us
    unnamed x1, local copies, waits for them, and re-layouts  3.16 us

profile of v3, /device:TPU:0, one launch (start us, length us, event | category | flops | bytes accessed | tf_op | source)
XLA Modules:
  0.0 105.4 jit_solution(6267659279999774456)
XLA Ops:
  0.0 0.9 reshape.3
  0.9 0.8 copy.6
  1.8 100.5 %shard_map.46 = bf16[512,2048]{1,0:T(8,128)(2,1)} custom-call(bf16[512,2048]{1,0:T(8,128)(2,1)} %tokens_hbm.1, bf16[128,3072]{1,0:T(8,128)(2,1)} %w_ref.1, bf16[64,2048]{1,0:T(8,128)(2,1)} %wo_ref.1, f32[512,56]{1,0:T(8,128)} %bitcast.1), custom_call_target="tpu_custom_call" | custom-call | tf_op jit(solution)/shard_map/pallas_call | solution.py:442
  102.3 3.2 %copy.8 = bf16[512,2048]{1,0:T(8,128)(2,1)} copy(bf16[512,2048]{1,0:T(8,128)(2,1)} %shard_map.46) | data formatting | bytes 4194304

commit v4 on v3

--- a/solution.py
+++ b/solution.py
@@ -57,7 +57,7 @@
 
 
 def relay_columns(columns, has_x, share):
-    return (columns // share) // 128 * 128 if has_x else 0
+    return (columns * share // 8) // 128 * 128 if has_x else 0
 
 
 class Gather:
@@ -158,10 +158,11 @@
                 for offset in self.complete(step - 1):
                     use(self.at.chip_at(offset))
             yield
-        for offset in self.complete(self.last - 1):
+        offsets = self.complete(self.last - 1)
+        before_end()
+        for offset in offsets:
             use(self.at.chip_at(offset))
         self.arrive(self.last)
-        before_end()
         yield
         for offset in self.complete(self.last):
             use(self.at.chip_at(offset))

time: 106 us -> 106 us (level)
  no operation moved by 1% of the time
where the time goes in v4:
time: 106 us; the launch traced here: 105 us
  Pallas kernels  100 us (94%)
  local copies, waits for them, and re-layouts  4.93 us (5%)
    pallas_call x1, Pallas kernels, on_device(): pl.pallas_call(functools.partial(layer_kernel, groups, seqs), out_shape=j...  100 us
    unnamed x1, local copies, waits for them, and re-layouts  3.16 us

profile of v4, /device:TPU:0, one launch (start us, length us, event | category | flops | bytes accessed | tf_op | source)
XLA Modules:
  0.0 105.0 jit_solution(13985232065120866840)
XLA Ops:
  0.0 0.9 reshape.3
  0.9 0.8 copy.6
  1.8 100.1 %shard_map.46 = bf16[512,2048]{1,0:T(8,128)(2,1)} custom-call(bf16[512,2048]{1,0:T(8,128)(2,1)} %tokens_hbm.1, bf16[128,3072]{1,0:T(8,128)(2,1)} %w_ref.1, bf16[64,2048]{1,0:T(8,128)(2,1)} %wo_ref.1, f32[512,56]{1,0:T(8,128)} %bitcast.1), custom_call_target="tpu_custom_call" | custom-call | tf_op jit(solution)/shard_map/pallas_call | solution.py:443
  101.9 3.2 %copy.8 = bf16[512,2048]{1,0:T(8,128)(2,1)} copy(bf16[512,2048]{1,0:T(8,128)(2,1)} %shard_map.46) | data formatting | bytes 4194304
